TPU v7x, 256 devices: a whole 4x4x8 slice. The times are simulated.
256 devices in a mesh: dp: 4 (over x), blk: 16 (over z_lo, y, core), mp: 4 (over z_hi).
Axes of the slice: x: 4, y: 4, z: 8 (z_hi: 4, z_lo: 2; z = z_hi * 2 + z_lo), core: 2. Of those that a mesh axis runs over, the one named last changes fastest.
Arguments:
- tokens: bfloat16 [16384, 7168], P('dp', ('blk', 'mp')), may hold values from -6 to 6
- trainer_q: float32 [3584, 7168], P(('mp', 'blk'), 'dp'), may hold values from -0.0625 to 0.0625
- kv_pool: bfloat16 [2, 8192, 3584], P(None, ('dp', 'blk'), 'mp')
- prompt_kv: bfloat16 [2, 16384, 3584], P(None, ('dp', 'blk'), 'mp'), may hold values from -15 to 15
- page_table: int32 [64, 64], P(('dp', 'blk')), may hold values from 0 to 127, as said below
- page_count: int32 [64], P(('dp', 'blk')), may hold values from 1 to 64
- prompt_len: int32 [64], P(('dp', 'blk')), may hold values from 64 to 256
Outputs:
- server_q: bfloat16 [3584, 7168], P('mp', 'blk')
- attn_out: bfloat16 [16384, 3584], P(('dp', 'blk'), 'mp')
Inputs may be any that keep to these rules, and one draw needn't show every extreme that they name: `page_table`: the entries of a row are distinct page numbers of the request's group.
All inputs are finite; a program needn't handle non-finite values.
Results may differ from a plain program's by a relative error of at most 0.012.
The roundings to bfloat16 on the way count: a program that leaves them out, or rounds other values in their place, can miss the bound.
Values may be sent and summed in bfloat16 or wider, within the bound.
A program may use at most 128 MiB of HBM per device.

v0:
```python
import jax
import jax.numpy as jnp
from jax import lax
from jax.sharding import PartitionSpec as P

HD = 224
PAGE = 16


def attend_block(softmax_state, query_heads, key_heads, value_heads, key_mask):
    running_max, row_total, weighted = softmax_state
    scores = jnp.einsum(
        "thd,khd->htk", query_heads, key_heads, preferred_element_type=jnp.float32
    ) * HD ** (-0.5)
    scores = jnp.where(key_mask[None], scores, -1e30)
    new_max = jnp.maximum(running_max, jnp.max(scores, axis=2))
    weights = jnp.where(key_mask[None], jnp.exp(scores - new_max[:, :, None]), 0.0)
    factor = jnp.exp(running_max - new_max)
    row_total = row_total * factor + jnp.sum(weights, axis=2)
    weighted = weighted * factor[:, :, None] + jnp.einsum(
        "htk,khd->htd",
        weights.astype(jnp.bfloat16),
        value_heads,
        preferred_element_type=jnp.float32,
    )
    return (new_max, row_total, weighted)


def body(tokens, trainer_q, kv_pool, prompt_kv, page_table, page_count, prompt_len):
    blk_size = lax.axis_size("blk")
    mp_size = lax.axis_size("mp")
    dp_size = lax.axis_size("dp")
    g = lax.axis_index("dp")
    own_piece = trainer_q.astype(jnp.bfloat16)
    received = jnp.stack(
        [own_piece]
        + [
            lax.ppermute(own_piece, "dp", [(i, (i + j) % dp_size) for i in range(dp_size)])
            for j in range(1, dp_size)
        ]
    )
    ordered = jnp.take(received, (g - jnp.arange(dp_size)) % dp_size, axis=0)
    trainer_rows = jnp.transpose(ordered, (1, 0, 2)).reshape(own_piece.shape[0], -1)
    head_weights = lax.all_gather(trainer_rows, "blk", axis=0, tiled=True)
    head_width, model_width = head_weights.shape
    block_cols = model_width // blk_size
    server_q = lax.dynamic_slice_in_dim(
        head_weights, lax.axis_index("blk") * block_cols, block_cols, axis=1
    )
    group_rows, piece_cols = tokens.shape
    own_rows = group_rows // blk_size
    pieces = tokens.reshape(blk_size, 1, own_rows, piece_cols)
    pieces = jnp.broadcast_to(pieces, (blk_size, mp_size, own_rows, piece_cols))
    pieces = pieces.reshape(blk_size * mp_size, own_rows, piece_cols)
    pieces = lax.all_to_all(pieces, ("blk", "mp"), 0, 0, tiled=True)
    token_local = jnp.transpose(pieces, (1, 0, 2)).reshape(own_rows, -1)
    queries = jnp.einsum("td,hd->th", token_local, head_weights, preferred_element_type=jnp.float32)
    queries = queries.astype(jnp.bfloat16)
    head_count = head_width // HD
    query_heads = queries.reshape(own_rows, head_count, HD)
    length = prompt_len[0]
    row_pages = page_table[0]
    live_slots = jnp.arange(row_pages.shape[0], dtype=jnp.int32) < page_count[0]
    row_index = jnp.arange(own_rows, dtype=jnp.int32)
    own_mask = (row_index[None, :] <= row_index[:, None]) & (row_index[None, :] < length)
    softmax_state = (
        jnp.full((head_count, own_rows), -1e30, jnp.float32),
        jnp.zeros((head_count, own_rows), jnp.float32),
        jnp.zeros((head_count, own_rows, HD), jnp.float32),
    )
    softmax_state = attend_block(
        softmax_state,
        query_heads,
        prompt_kv[0].reshape(own_rows, head_count, HD),
        prompt_kv[1].reshape(own_rows, head_count, HD),
        own_mask,
    )
    shard_piece = lax.all_gather(kv_pool, "blk", axis=1, tiled=True)
    key_count = shard_piece.shape[1]
    page_ids = jnp.arange(key_count, dtype=jnp.int32) // PAGE
    page_used = jnp.any((row_pages[None, :] == page_ids[:, None]) & live_slots[None, :], axis=1)
    key_mask = jnp.broadcast_to(page_used[None, :], (own_rows, key_count))
    running_max, row_total, weighted = attend_block(
        softmax_state,
        query_heads,
        shard_piece[0].reshape(key_count, head_count, HD),
        shard_piece[1].reshape(key_count, head_count, HD),
        key_mask,
    )
    mixed = weighted / row_total[:, :, None]
    mixed = jnp.where((row_index < length)[None, :, None], mixed, 0.0)
    mixed = jnp.transpose(mixed, (1, 0, 2)).reshape(own_rows, head_width).astype(jnp.bfloat16)
    return (server_q, mixed)


def solution(mesh):
    in_specs = (
        P("dp", ("blk", "mp")),
        P(("mp", "blk"), "dp"),
        P(None, ("dp", "blk"), "mp"),
        P(None, ("dp", "blk"), "mp"),
        P(("dp", "blk"), None),
        P(("dp", "blk")),
        P(("dp", "blk")),
    )
    out_specs = (P("mp", "blk"), P(("dp", "blk"), "mp"))
    return jax.shard_map(body, mesh=mesh, in_specs=in_specs, out_specs=out_specs, check_vma=False)
```

profile of v0, /device:TPU:1, one launch (start us, length us, event | category | flops | bytes accessed | tf_op | source)
XLA Modules:
  0.0 230.1 jit_solution(18045067984531203395)
XLA Ops:
  7.2 0.0 copy-start.2
  7.2 0.0 all-gather.5.cloned.1.call-start
  7.2 0.7 all-gather.5.cloned.1.call-update
  7.9 0.0 all-gather.3.cloned.1.call-start
  8.0 1.0 convert_element_type.21
  9.0 3.4 %collective-permute-start.2 = (bf16[56,1792]{1,0:T(8,128)(2,1)S(1)}, bf16[56,1792]{1,0:T(8,128)(2,1)S(1)}, u32[]{:S(2)}, u32[]{:S(2)}) collective-permute-start(bf16[56,1792]{1,0:T(8,128)(2,1)S(1)} %convert_element_type.21), channel_id=1, source_target_pairs={{0,192},{64,0},{128,64},{192,128},{1,193},{65,1},{129,65},{193,129... | collective-permute-start | bytes 602120 | tf_op jit(solution)/shard_map/ppermute | solution.py:38
  12.4 0.5 collective-permute-start.1
  12.9 0.6 collective-permute-start
  13.5 1.0 convert_bitcast_fusion
  14.6 3.7 %collective-permute-done.2 = bf16[56,1792]{1,0:T(8,128)(2,1)S(1)} collective-permute-done((bf16[56,1792]{1,0:T(8,128)(2,1)S(1)}, bf16[56,1792]{1,0:T(8,128)(2,1)S(1)}, u32[]{:S(2)}, u32[]{:S(2)}) %collective-permute-start.2) | collective-permute-done | bytes 200736 | tf_op jit(solution)/shard_map/ppermute | solution.py:38
  18.2 1.2 collective-permute-done.1
  19.5 5.6 %collective-permute-done = bf16[56,1792]{1,0:T(8,128)(2,1)S(1)} collective-permute-done((bf16[56,1792]{1,0:T(8,128)(2,1)S(1)}, bf16[56,1792]{1,0:T(8,128)(2,1)S(1)}, u32[]{:S(2)}, u32[]{:S(2)}) %collective-permute-start) | collective-permute-done | bytes 200736 | tf_op jit(solution)/shard_map/ppermute | solution.py:38
  25.1 0.1 pad_maximum_fusion
  25.2 0.6 gather_fusion
  25.8 0.1 select_bitcast_fusion
  25.9 0.0 copy-start.3
  26.0 0.9 copy.45
  26.9 0.0 all-gather.3.cloned.1.call-update
  26.9 0.0 copy-done.2
  26.9 0.0 copy-start.4
  27.0 0.1 copy.47
  27.0 2.2 broadcast_in_dim.94
  29.2 12.3 %all-to-all-start = ((bf16[64,256,112]{1,2,0:T(8,128)(2,1)}), bf16[64,256,112]{1,2,0:T(8,128)(2,1)}, u32[]{:S(2)}, u32[]{:S(2)}) async-start(bf16[64,256,112]{1,2,0:T(8,128)(2,1)} %bitcast.77), calls=%async_computation | async-start | bytes 7340032 | tf_op jit(solution)/shard_map/all_to_all | solution.py:55
  42.2 0.0 copy-done.3
  42.2 0.1 fusion.40
  42.3 0.2 copy.36
  43.1 0.2 copy.37
  43.4 0.0 copy-done.4
  43.4 0.2 and_reduce_fusion
  43.6 0.1 fusion.22
  43.7 66.8 %all-gather.5.cloned.1.call-done = bf16[2,2048,896]{2,1,0:T(8,128)(2,1)} async-done(((bf16[2,128,896]{2,1,0:T(8,128)(2,1)}), bf16[2,2048,896]{2,1,0:T(8,128)(2,1)}) %all-gather.5.cloned.1.call-update) | async-done | bytes 7340048 | tf_op jit(solution)/shard_map/all_gather | solution.py:78
  110.5 6.7 %fusion.39 = (bf16[1,2048,896]{2,1,0:T(8,128)(2,1)}, bf16[1,2048,896]{2,1,0:T(8,128)(2,1)}) fusion(bf16[2,2048,896]{2,1,0:T(8,128)(2,1)} %all-gather.5.cloned.1.call-done), kind=kLoop, calls=%fused_computation.68 | loop fusion | bytes 14680064 | tf_op jit(solution)/shard_map/slice | solution.py:86
  117.2 6.2 %copy.40 = bf16[1,2048,896]{1,2,0:T(8,128)(2,1)} copy(bf16[1,2048,896]{2,1,0:T(8,128)(2,1)} %get-tuple-element.13) | data formatting | bytes 7340032 | tf_op jit(solution)/shard_map/slice | solution.py:87
  123.4 6.2 %copy.39 = bf16[1,2048,896]{1,2,0:T(8,128)(2,1)} copy(bf16[1,2048,896]{2,1,0:T(8,128)(2,1)} %get-tuple-element.12) | data formatting | bytes 7340032 | tf_op jit(solution)/shard_map/slice | solution.py:86
  129.6 73.3 %all-gather.3.cloned.1.call-done = bf16[896,7168]{1,0:T(8,128)(2,1)} async-done(((bf16[56,7168]{1,0:T(8,128)(2,1)}), bf16[896,7168]{1,0:T(8,128)(2,1)}) %all-gather.3.cloned.1.call-update) | async-done | bytes 12845072 | tf_op jit(solution)/shard_map/all_gather | solution.py:44
  202.8 1.6 constant_dynamic-slice_fusion
  204.5 1.2 copy.41
  205.7 0.0 all-to-all-done
  205.7 9.3 %convolution_convert_fusion = bf16[896,256]{1,0:T(8,128)(2,1)S(1)} fusion(bf16[896,7168]{1,0:T(8,128)(2,1)} %all-gather.3.cloned.1.call-done, bf16[256,7168]{0,1:T(8,128)(2,1)} %bitcast.9), kind=kOutput, calls=%fused_computation.17 | convolution fusion | flops 3288563712 | bytes 16973824 | tf_op jit(solution)/shard_map/td,hd->th/dot_general | solution.py:57
  215.0 0.0 copy-done
  215.0 0.0 copy-start.1
  215.1 1.9 fusion
  216.9 0.4 fusion.41
  217.3 2.2 fusion.1
  219.5 2.1 fusion.7
  221.7 0.2 fusion.16
  221.9 0.4 fusion.15
  222.3 1.0 copy.42
  (10 shorter events, 0.1 us)
Async XLA Ops:
  7.2 19.8 %copy-start.2 = (bf16[4096,112]{0,1:T(8,128)(2,1)S(1)}, bf16[4096,112]{0,1:T(8,128)(2,1)}, u32[]{:S(2)}) copy-start(bf16[4096,112]{0,1:T(8,128)(2,1)} %param.7) | copy-start | bytes 2752516
  7.2 103.3 %all-gather.5.cloned.1.call-start = ((), (), s32[]{:S(2)}) async-start(), calls=%async_computation.2 | async-start | bytes 7798784 | tf_op jit(solution)/shard_map/all_gather | solution.py:78
  7.9 194.9 %all-gather.3.cloned.1.call-start = ((), (), s32[]{:S(2)}) async-start(), calls=%async_computation.1 | async-start | bytes 13647872 | tf_op jit(solution)/shard_map/all_gather | solution.py:44
  9.0 9.2 %collective-permute-start.2 = (bf16[56,1792]{1,0:T(8,128)(2,1)S(1)}, bf16[56,1792]{1,0:T(8,128)(2,1)S(1)}, u32[]{:S(2)}, u32[]{:S(2)}) collective-permute-start(bf16[56,1792]{1,0:T(8,128)(2,1)S(1)} %convert_element_type.21), channel_id=1, source_target_pairs={{0,192},{64,0},{128,64},{192,128},{1,193},{65,1},{129,65},{193,129... | collective-permute-start | bytes 602120 | tf_op jit(solution)/shard_map/ppermute | solution.py:38
  12.4 7.1 %collective-permute-start.1 = (bf16[56,1792]{1,0:T(8,128)(2,1)S(1)}, bf16[56,1792]{1,0:T(8,128)(2,1)S(1)}, u32[]{:S(2)}, u32[]{:S(2)}) collective-permute-start(bf16[56,1792]{1,0:T(8,128)(2,1)S(1)} %convert_element_type.21), channel_id=1, source_target_pairs={{0,128},{64,192},{128,0},{192,64},{1,129},{65,193},{129,1},{193,65... | collective-permute-start | bytes 602120 | tf_op jit(solution)/shard_map/ppermute | solution.py:38
  12.9 12.2 %collective-permute-start = (bf16[56,1792]{1,0:T(8,128)(2,1)S(1)}, bf16[56,1792]{1,0:T(8,128)(2,1)S(1)}, u32[]{:S(2)}, u32[]{:S(2)}) collective-permute-start(bf16[56,1792]{1,0:T(8,128)(2,1)S(1)} %convert_element_type.21), channel_id=1, source_target_pairs={{0,64},{64,128},{128,192},{192,0},{1,65},{65,129},{129,193},{193,1... | collective-permute-start | bytes 602120 | tf_op jit(solution)/shard_map/ppermute | solution.py:38
  25.9 16.2 %copy-start.3 = (bf16[2,256,896]{2,1,0:T(8,128)(2,1)S(1)}, bf16[2,256,896]{2,1,0:T(8,128)(2,1)}, u32[]{:S(2)}) copy-start(bf16[2,256,896]{2,1,0:T(8,128)(2,1)} %param.10) | copy-start | bytes 2752516
  26.9 16.5 %copy-start.4 = (s32[1,64]{1,0:T(1,128)S(1)}, s32[1,64]{1,0:T(1,128)}, u32[]{:S(2)}) copy-start(s32[1,64]{1,0:T(1,128)} %param.11) | copy-start | bytes 772
  29.2 176.5 %all-to-all-start = ((bf16[64,256,112]{1,2,0:T(8,128)(2,1)}), bf16[64,256,112]{1,2,0:T(8,128)(2,1)}, u32[]{:S(2)}, u32[]{:S(2)}) async-start(bf16[64,256,112]{1,2,0:T(8,128)(2,1)} %bitcast.77), calls=%async_computation | async-start | bytes 7340032 | tf_op jit(solution)/shard_map/all_to_all | solution.py:55
  205.7 9.3 %copy-start = (bf16[1,2048,896]{1,2,0:T(8,128)(2,1)S(1)}, bf16[1,2048,896]{1,2,0:T(8,128)(2,1)}, u32[]{:S(2)}) copy-start(bf16[1,2048,896]{1,2,0:T(8,128)(2,1)} %copy.39) | copy-start | bytes 11010052
  215.0 4.5 %copy-start.1 = (bf16[1,2048,896]{1,2,0:T(8,128)(2,1)S(1)}, bf16[1,2048,896]{1,2,0:T(8,128)(2,1)}, u32[]{:S(2)}) copy-start(bf16[1,2048,896]{1,2,0:T(8,128)(2,1)} %copy.40) | copy-start | bytes 11010052
Sparse Core Ops, SparseCore 0:
  9.8 100.6 all-gather.4
  112.9 89.8 all-gather.2
where the time goes:
time: 231 us; the launch traced here: 230 us
  waiting for transfers between devices  151 us (65%)
  local copies, waits for them, and re-layouts  27.2 us (12%)
  starting transfers between devices  16.9 us (7%)
  between operations  15.6 us (7%)
  matrix products  14.1 us (6%)
  other arithmetic  5.04 us (2%)
    all_gather x1, waiting for transfers between devices, body(): head_weights = lax.all_gather(trainer_rows, 'blk', axis=0, tiled=True)  73.3 us
    all_gather x1, waiting for transfers between devices, body(): shard_piece = lax.all_gather(kv_pool, 'blk', axis=1, tiled=True)  66.8 us
    slice x2, local copies, waits for them, and re-layouts, body(): shard_piece[0].reshape(key_count, head_count, HD)  12.9 us
    all_to_all x1, starting transfers between devices, body(): pieces = lax.all_to_all(pieces, ('blk', 'mp'), 0, 0, tiled=True)  12.3 us
    ppermute x3, waiting for transfers between devices, body(): lax.ppermute(own_piece, 'dp', [(i, (i + j) % dp_size) for i in range(dp_s...  10.5 us
    dot_general x1, matrix products, body(): jnp.einsum('td,hd->th', token_local, head_weights, preferred_element_type...  9.31 us
    slice x1, local copies, waits for them, and re-layouts, body(): shard_piece[1].reshape(key_count, head_count, HD)  6.17 us
  transfers between devices with their start and end apart: 6, of which 5 were waited for; matrix products, arithmetic and copies ran while one was open for 13% of the time, Pallas kernels for 0%

commit v1 on v0

--- a/solution.py
+++ b/solution.py
@@ -1,3 +1,4 @@
+import functools
 import jax
 import jax.numpy as jnp
 from jax import lax
@@ -5,6 +6,19 @@
 
 HD = 224
 PAGE = 16
+
+
+def copies_save(z, axis_tag):
+    state_next = jnp.concatenate(
+        lax.all_to_all(
+            jnp.stack([z] * lax.axis_size(axis_tag)), axis_tag, split_axis=0, concat_axis=0
+        ),
+        axis=0,
+    )
+    return state_next
+
+
+_order_unit = functools.partial(copies_save, axis_tag="blk")
 
 
 def attend_block(softmax_state, query_heads, key_heads, value_heads, key_mask):
@@ -41,7 +55,7 @@
     )
     ordered = jnp.take(received, (g - jnp.arange(dp_size)) % dp_size, axis=0)
     trainer_rows = jnp.transpose(ordered, (1, 0, 2)).reshape(own_piece.shape[0], -1)
-    head_weights = lax.all_gather(trainer_rows, "blk", axis=0, tiled=True)
+    head_weights = _order_unit(trainer_rows)
     head_width, model_width = head_weights.shape
     block_cols = model_width // blk_size
     server_q = lax.dynamic_slice_in_dim(

time: 231 us -> 346 us (1.50)
  waiting for transfers between devices: 151 us -> 255 us
  starting transfers between devices: 16.9 us -> 22.6 us
  local copies, waits for them, and re-layouts: 27.2 us -> 32.3 us
    all_to_all x0 -> x1, waiting for transfers between devices: none -> 183 us  [copies_save(): lax.all_to_all(jnp.stack([z] * lax.axis_size(axis_tag)), axis_tag, split_...]
    all_gather x1 -> x0, waiting for transfers between devices: 73.3 us -> none  [body(): head_weights = lax.all_gather(trainer_rows, 'blk', axis=0, tiled=True)]
    all_gather x1, waiting for transfers between devices: 66.8 us -> 0.02 us  [body(): shard_piece = lax.all_gather(kv_pool, 'blk', axis=1, tiled=True)]
    all_to_all x1, waiting for transfers between devices: 0.01 us -> 60.8 us  [body(): pieces = lax.all_to_all(pieces, ('blk', 'mp'), 0, 0, tiled=True)]
    all_to_all x0 -> x1, starting transfers between devices: none -> 6.46 us  [copies_save(): lax.all_to_all(jnp.stack([z] * lax.axis_size(axis_tag)), axis_tag, split_...]
    another operation x0 -> x2, local copies, waits for them, and re-layouts: none -> 6.26 us  [copies_save(): jnp.stack([z] * lax.axis_size(axis_tag))]
  transfers between devices with their start and end apart: 6 -> 6, of which waited for: 5 -> 5; matrix products, arithmetic and copies ran while one was open for 13% -> 7% of each run, Pallas kernels for 0% -> 0%
where the time goes in v1:
time: 346 us; the launch traced here: 345 us
  waiting for transfers between devices  255 us (74%)
  local copies, waits for them, and re-layouts  32.3 us (9%)
  starting transfers between devices  22.6 us (7%)
  between operations  15.6 us (5%)
  matrix products  14.1 us (4%)
  other arithmetic  5.04 us (1%)
    all_to_all x1, waiting for transfers between devices, copies_save(): lax.all_to_all(jnp.stack([z] * lax.axis_size(axis_tag)), axis_tag, split_...  183 us
    all_to_all x1, waiting for transfers between devices, body(): pieces = lax.all_to_all(pieces, ('blk', 'mp'), 0, 0, tiled=True)  60.8 us
    slice x2, local copies, waits for them, and re-layouts, body(): shard_piece[0].reshape(key_count, head_count, HD)  12.8 us
    all_to_all x1, starting transfers between devices, body(): pieces = lax.all_to_all(pieces, ('blk', 'mp'), 0, 0, tiled=True)  11.6 us
    ppermute x3, waiting for transfers between devices, body(): lax.ppermute(own_piece, 'dp', [(i, (i + j) % dp_size) for i in range(dp_s...  10.5 us
    dot_general x1, matrix products, body(): jnp.einsum('td,hd->th', token_local, head_weights, preferred_element_type...  9.31 us
  transfers between devices with their start and end apart: 6, of which 5 were waited for; matrix products, arithmetic and copies ran while one was open for 7% of the time, Pallas kernels for 0%

profile of v1, /device:TPU:1, one launch (start us, length us, event | category | flops | bytes accessed | tf_op | source)
XLA Modules:
  0.0 345.0 jit_solution(10040140252083589940)
XLA Ops:
  7.2 1.0 convert_element_type.21
  8.2 3.4 collective-permute-start.2
  11.6 0.5 collective-permute-start.1
  12.1 0.6 collective-permute-start
  12.7 1.0 convert_bitcast_fusion
  13.8 3.7 %collective-permute-done.2 = bf16[56,1792]{1,0:T(8,128)(2,1)S(1)} collective-permute-done((bf16[56,1792]{1,0:T(8,128)(2,1)S(1)}, bf16[56,1792]{1,0:T(8,128)(2,1)S(1)}, u32[]{:S(2)}, u32[]{:S(2)}) %collective-permute-start.2) | collective-permute-done | bytes 200736 | tf_op jit(solution)/shard_map/ppermute | solution.py:52
  17.4 1.2 collective-permute-done.1
  18.7 5.6 %collective-permute-done = bf16[56,1792]{1,0:T(8,128)(2,1)S(1)} collective-permute-done((bf16[56,1792]{1,0:T(8,128)(2,1)S(1)}, bf16[56,1792]{1,0:T(8,128)(2,1)S(1)}, u32[]{:S(2)}, u32[]{:S(2)}) %collective-permute-start) | collective-permute-done | bytes 200736 | tf_op jit(solution)/shard_map/ppermute | solution.py:52
  24.3 0.1 pad_maximum_fusion
  24.4 0.6 gather_fusion
  25.0 0.1 select_bitcast_fusion
  25.2 0.1 copy.36
  25.2 6.2 %stack.23 = bf16[16,56,7168]{2,1,0:T(8,128)(2,1)} broadcast(bf16[56,7168]{1,0:T(8,128)(2,1)S(1)} %bitcast.82), dimensions={1,2} | broadcast | bytes 13647872 | tf_op jit(solution)/shard_map/stack | solution.py:14
  31.4 0.0 copy-start.2
  31.4 6.5 %all-to-all-start = ((bf16[16,56,7168]{2,1,0:T(8,128)(2,1)}), bf16[16,56,7168]{2,1,0:T(8,128)(2,1)}, u32[]{:S(2)}, u32[]{:S(2)}) async-start(bf16[16,56,7168]{2,1,0:T(8,128)(2,1)} %stack.23), calls=%async_computation | async-start | bytes 25690112 | tf_op jit(solution)/shard_map/all_to_all | solution.py:13
  37.9 0.0 all-gather.2.cloned.1.call-start
  37.9 0.7 all-gather.2.cloned.1.call-update
  38.6 0.0 copy-done.2
  38.6 0.0 copy-start.4
  38.6 0.1 copy.38
  38.7 183.3 %all-to-all-done = bf16[16,56,7168]{2,1,0:T(8,128)(2,1)} async-done(((bf16[16,56,7168]{2,1,0:T(8,128)(2,1)}), bf16[16,56,7168]{2,1,0:T(8,128)(2,1)}, u32[]{:S(2)}, u32[]{:S(2)}) %all-to-all-start) | async-done | bytes 12845088 | tf_op jit(solution)/shard_map/all_to_all | solution.py:13
  222.0 2.1 broadcast_in_dim.94
  224.1 11.6 %all-to-all-start.1 = ((bf16[64,256,112]{1,2,0:T(8,128)(2,1)}), bf16[64,256,112]{1,2,0:T(8,128)(2,1)}, u32[]{:S(2)}, u32[]{:S(2)}) async-start(bf16[64,256,112]{1,2,0:T(8,128)(2,1)} %bitcast.78), calls=%async_computation.1 | async-start | bytes 7340032 | tf_op jit(solution)/shard_map/all_to_all | solution.py:69
  236.4 0.0 copy-done.3
  236.4 0.1 fusion.40
  236.5 0.2 copy.27
  237.3 0.2 copy.28
  237.6 0.0 copy-done.4
  237.6 0.2 and_reduce_fusion
  237.8 0.1 fusion.22
  237.9 0.0 all-gather.2.cloned.1.call-done
  237.9 6.6 %fusion.39 = (bf16[1,2048,896]{2,1,0:T(8,128)(2,1)}, bf16[1,2048,896]{2,1,0:T(8,128)(2,1)}) fusion(bf16[2,2048,896]{2,1,0:T(8,128)(2,1)} %all-gather.2.cloned.1.call-done), kind=kLoop, calls=%fused_computation.68 | loop fusion | bytes 14680064 | tf_op jit(solution)/shard_map/slice | solution.py:100
  244.5 6.1 %copy.31 = bf16[1,2048,896]{1,2,0:T(8,128)(2,1)} copy(bf16[1,2048,896]{2,1,0:T(8,128)(2,1)} %get-tuple-element.11) | data formatting | bytes 7340032 | tf_op jit(solution)/shard_map/slice | solution.py:101
  250.7 6.2 %copy.30 = bf16[1,2048,896]{1,2,0:T(8,128)(2,1)} copy(bf16[1,2048,896]{2,1,0:T(8,128)(2,1)} %get-tuple-element.10) | data formatting | bytes 7340032 | tf_op jit(solution)/shard_map/slice | solution.py:100
  256.8 1.6 constant_dynamic-slice_fusion
  258.5 1.2 copy.32
  259.7 60.8 %all-to-all-done.1 = bf16[64,256,112]{1,2,0:T(8,128)(2,1)} async-done(((bf16[64,256,112]{1,2,0:T(8,128)(2,1)}), bf16[64,256,112]{1,2,0:T(8,128)(2,1)}, u32[]{:S(2)}, u32[]{:S(2)}) %all-to-all-start.1) | async-done | bytes 3670048 | tf_op jit(solution)/shard_map/all_to_all | solution.py:69
  320.6 9.3 %convolution_convert_fusion = bf16[896,256]{1,0:T(8,128)(2,1)S(1)} fusion(bf16[896,7168]{1,0:T(8,128)(2,1)} %bitcast.6, bf16[256,7168]{0,1:T(8,128)(2,1)} %bitcast.10), kind=kOutput, calls=%fused_computation.17 | convolution fusion | flops 3288563712 | bytes 16973824 | tf_op jit(solution)/shard_map/td,hd->th/dot_general | solution.py:71
  329.9 0.0 copy-done
  329.9 0.0 copy-start.1
  329.9 1.9 fusion
  331.8 0.4 fusion.41
  332.2 2.2 fusion.1
  334.4 0.0 copy-done.1
  334.4 2.1 fusion.7
  336.5 0.2 fusion.16
  336.7 0.4 fusion.15
  337.2 1.0 copy.33
  (10 shorter events, 0.1 us)
Async XLA Ops:
  8.2 9.2 %collective-permute-start.2 = (bf16[56,1792]{1,0:T(8,128)(2,1)S(1)}, bf16[56,1792]{1,0:T(8,128)(2,1)S(1)}, u32[]{:S(2)}, u32[]{:S(2)}) collective-permute-start(bf16[56,1792]{1,0:T(8,128)(2,1)S(1)} %convert_element_type.21), channel_id=1, source_target_pairs={{0,192},{64,0},{128,64},{192,128},{1,193},{65,1},{129,65},{193,129... | collective-permute-start | bytes 602120 | tf_op jit(solution)/shard_map/ppermute | solution.py:52
  11.6 7.1 %collective-permute-start.1 = (bf16[56,1792]{1,0:T(8,128)(2,1)S(1)}, bf16[56,1792]{1,0:T(8,128)(2,1)S(1)}, u32[]{:S(2)}, u32[]{:S(2)}) collective-permute-start(bf16[56,1792]{1,0:T(8,128)(2,1)S(1)} %convert_element_type.21), channel_id=1, source_target_pairs={{0,128},{64,192},{128,0},{192,64},{1,129},{65,193},{129,1},{193,65... | collective-permute-start | bytes 602120 | tf_op jit(solution)/shard_map/ppermute | solution.py:52
  12.1 12.2 %collective-permute-start = (bf16[56,1792]{1,0:T(8,128)(2,1)S(1)}, bf16[56,1792]{1,0:T(8,128)(2,1)S(1)}, u32[]{:S(2)}, u32[]{:S(2)}) collective-permute-start(bf16[56,1792]{1,0:T(8,128)(2,1)S(1)} %convert_element_type.21), channel_id=1, source_target_pairs={{0,64},{64,128},{128,192},{192,0},{1,65},{65,129},{129,193},{193,1... | collective-permute-start | bytes 602120 | tf_op jit(solution)/shard_map/ppermute | solution.py:52
  31.4 7.2 %copy-start.2 = (bf16[4096,112]{0,1:T(8,128)(2,1)S(1)}, bf16[4096,112]{0,1:T(8,128)(2,1)}, u32[]{:S(2)}) copy-start(bf16[4096,112]{0,1:T(8,128)(2,1)} %param.7) | copy-start | bytes 2752516
  31.4 190.6 %all-to-all-start = ((bf16[16,56,7168]{2,1,0:T(8,128)(2,1)}), bf16[16,56,7168]{2,1,0:T(8,128)(2,1)}, u32[]{:S(2)}, u32[]{:S(2)}) async-start(bf16[16,56,7168]{2,1,0:T(8,128)(2,1)} %stack.23), calls=%async_computation | async-start | bytes 25690112 | tf_op jit(solution)/shard_map/all_to_all | solution.py:13
  37.9 198.5 %copy-start.3 = (bf16[2,256,896]{2,1,0:T(8,128)(2,1)S(1)}, bf16[2,256,896]{2,1,0:T(8,128)(2,1)}, u32[]{:S(2)}) copy-start(bf16[2,256,896]{2,1,0:T(8,128)(2,1)} %param.10) | copy-start | bytes 2752516
  37.9 200.0 %all-gather.2.cloned.1.call-start = ((), (), s32[]{:S(2)}) async-start(), calls=%async_computation.2 | async-start | bytes 7798784 | tf_op jit(solution)/shard_map/all_gather | solution.py:92
  38.6 199.0 %copy-start.4 = (s32[1,64]{1,0:T(1,128)S(1)}, s32[1,64]{1,0:T(1,128)}, u32[]{:S(2)}) copy-start(s32[1,64]{1,0:T(1,128)} %param.11) | copy-start | bytes 772
  224.1 96.5 %all-to-all-start.1 = ((bf16[64,256,112]{1,2,0:T(8,128)(2,1)}), bf16[64,256,112]{1,2,0:T(8,128)(2,1)}, u32[]{:S(2)}, u32[]{:S(2)}) async-start(bf16[64,256,112]{1,2,0:T(8,128)(2,1)} %bitcast.78), calls=%async_computation.1 | async-start | bytes 7340032 | tf_op jit(solution)/shard_map/all_to_all | solution.py:69
  320.6 9.3 %copy-start = (bf16[1,2048,896]{1,2,0:T(8,128)(2,1)S(1)}, bf16[1,2048,896]{1,2,0:T(8,128)(2,1)}, u32[]{:S(2)}) copy-start(bf16[1,2048,896]{1,2,0:T(8,128)(2,1)} %copy.30) | copy-start | bytes 11010052
  329.9 4.5 %copy-start.1 = (bf16[1,2048,896]{1,2,0:T(8,128)(2,1)S(1)}, bf16[1,2048,896]{1,2,0:T(8,128)(2,1)}, u32[]{:S(2)}) copy-start(bf16[1,2048,896]{1,2,0:T(8,128)(2,1)} %copy.31) | copy-start | bytes 11010052
Sparse Core Ops, SparseCore 0:
  40.5 177.9 all-gather.1
